TPU v7x, 256 devices: a whole 4x4x8 slice. The times are simulated.
256 devices in a mesh: req: 32 (over z, y), mdl: 8 (over x, core).
Axes of the slice: x: 4, y: 4, z: 8, core: 2. Of those that a mesh axis runs over, the one named last changes fastest.
Arguments:
- stream: bfloat16 [24576, 1792], P('req'), may hold values from -6 to 6
- attention_projection_weight: bfloat16 [3, 1792, 1792], P(None, 'mdl'), may hold values from -0.125 to 0.125
- head_output_weight: bfloat16 [1792, 1792], P('mdl'), may hold values from -0.125 to 0.125
- adapter_down_maps: bfloat16 [64, 1792, 16], P('mdl'), may hold values from -0.125 to 0.125
- adapter_up_maps: bfloat16 [2, 1792, 1024], P(None, 'mdl'), may hold values from -1.5 to 1.5
- tenant_adapter_scale: float32 [4], replicated, may hold values from 0.5 to 2
- feedforward_norm_gain: bfloat16 [1792], replicated, may hold values from 0.099609375 to 1.8984375
- feedforward_weight: bfloat16 [3, 1792, 4864], P(None, 'req', 'mdl'), may hold values from -0.125 to 0.125
- prefix_cache_store: bfloat16 [1024, 2, 1792, 128], P('req', None, 'mdl'), may hold values from -140 to 140
- token_adapter_index: int32 [24576], P('req'), may hold values from 0 to 63
- request_token_lengths: int32 [32, 24], P('req'), may hold values from 1 to 192, 768 in all within a row
- request_tenant_index: int32 [768], P('req'), may hold values from 0 to 3
- last_page_holder: int32 [768, 1], replicated, may hold values from 0 to 31; in each aligned block of 24 rows (0 to 23, 24 to 47, ...) at most 2 rows name the same one
- holder_page_slot: int32 [768], replicated, may hold values from 0 to 31
- page_filled_rows: int32 [768], replicated, may hold values from 64 to 128
Outputs:
- layer_out: bfloat16 [24576, 1792], P(('req', 'mdl'))
Inputs may be any that keep to these rules, and one draw needn't show every extreme that they name: `last_page_holder`: within the rows of one index of req (aligned blocks of 24 rows) no holder is named more than 2 times, and one holder exactly 2 times in some blocks. `request_token_lengths`: each row sums to 768; its longest request has exactly 192 tokens.
All inputs are finite; a program needn't handle non-finite values.
Results may differ from a plain program's by a relative error of at most 0.025.
Values may be sent and summed in bfloat16 or wider, within the bound.
A program may use at most 128 MiB of HBM per device.

v0:
```python
import math
import jax
import jax.numpy as jnp
from jax import lax
from jax.sharding import PartitionSpec as P

HEAD_SIZE = 112
WINDOW = 64


def window_cols(one_page, fill_rows):
    return lax.dynamic_slice_in_dim(one_page, fill_rows - WINDOW, WINDOW, 2)


def per_device(
    stream,
    attention_projection_weight,
    head_output_weight,
    adapter_down_maps,
    adapter_up_maps,
    tenant_adapter_scale,
    feedforward_norm_gain,
    feedforward_weight,
    prefix_cache_store,
    token_adapter_index,
    request_token_lengths,
    request_tenant_index,
    last_page_holder,
    holder_page_slot,
    page_filled_rows,
):
    tok_count, model_width = stream.shape
    head_column_set = attention_projection_weight.shape[1]
    head_local = head_column_set // HEAD_SIZE
    req_per_dev = request_token_lengths.shape[1]
    rank_total_width = adapter_down_maps.shape[2]
    adapter_number = adapter_up_maps.shape[2] // rank_total_width
    req_devices = lax.axis_size("req")
    req_index = lax.axis_index("req")
    mdl_index = lax.axis_index("mdl")
    row_share = tok_count // lax.axis_size("mdl")
    cap_slots = max(2, (req_per_dev + req_devices - 1) // req_devices + 1)
    projected_rows = jnp.einsum(
        "td,kcd->ktc", stream, attention_projection_weight, preferred_element_type=jnp.float32
    )
    all_onehot = (
        token_adapter_index[:, None] == jnp.arange(adapter_number, dtype=jnp.int32)[None, :]
    )
    holder_count = adapter_down_maps.shape[0]
    holder_rank_rows = jnp.einsum(
        "qf,kfn->qkn", stream, adapter_down_maps, preferred_element_type=jnp.float32
    )
    held_onehot = (
        token_adapter_index[:, None]
        == (mdl_index * holder_count + jnp.arange(holder_count, dtype=jnp.int32))[None, :]
    )
    rank_part = jnp.sum(holder_rank_rows * held_onehot.astype(jnp.float32)[:, :, None], axis=1)
    rank_feat = lax.psum(rank_part.astype(jnp.bfloat16), "mdl")
    broadcast_result = (
        all_onehot.astype(jnp.bfloat16)[:, :, None] * rank_feat[:, None, :]
    ).reshape(tok_count, adapter_number * rank_total_width)
    adapter_column_set = jnp.einsum(
        "iu,pdu->ipd", broadcast_result, adapter_up_maps, preferred_element_type=jnp.float32
    )
    positions = jnp.arange(tok_count, dtype=jnp.int32)
    lengths_row = request_token_lengths[0]
    starts = jnp.cumsum(lengths_row) - lengths_row
    member = (positions[:, None] >= starts[None, :]) & (
        positions[:, None] < (starts + lengths_row)[None, :]
    )
    member_int = member.astype(jnp.int32)
    request_of = jnp.sum(member_int * jnp.arange(req_per_dev, dtype=jnp.int32)[None, :], axis=1)
    relative = positions - jnp.sum(member_int * starts[None, :], axis=1)
    tenant_hot = (
        request_tenant_index[:, None]
        == jnp.arange(tenant_adapter_scale.shape[0], dtype=jnp.int32)[None, :]
    ).astype(jnp.float32)
    request_scale = jnp.sum(tenant_hot * tenant_adapter_scale[None, :], axis=1)
    per_token_scale = jnp.sum(member.astype(jnp.float32) * request_scale[None, :], axis=1)[:, None]
    query_rows = (projected_rows[0] + per_token_scale * adapter_column_set[:, 0]).astype(
        jnp.bfloat16
    )
    key_rows = projected_rows[1].astype(jnp.bfloat16)
    value_row_block = (projected_rows[2] + per_token_scale * adapter_column_set[:, 1]).astype(
        jnp.bfloat16
    )
    owner_column = last_page_holder[:, 0]
    owner_table = owner_column.reshape(req_devices, req_per_dev)
    slot_table = holder_page_slot.reshape(req_devices, req_per_dev)
    owned = (owner_table == req_index).astype(jnp.int32)
    owned_rank = jnp.cumsum(owned, axis=1) - 1
    picked = owned[:, None, :] * (
        owned_rank[:, None, :] == jnp.arange(cap_slots, dtype=jnp.int32)[None, :, None]
    ).astype(jnp.int32)
    send_slot = jnp.sum(picked * slot_table[:, None, :], axis=2)
    my_owner = lax.dynamic_slice_in_dim(owner_column, req_index * req_per_dev, req_per_dev, 0)
    my_fill = lax.dynamic_slice_in_dim(page_filled_rows, req_index * req_per_dev, req_per_dev, 0)
    order_ids = jnp.arange(req_per_dev, dtype=jnp.int32)
    earlier = (my_owner[:, None] == my_owner[None, :]) & (order_ids[:, None] > order_ids[None, :])
    flat_pick = my_owner * cap_slots + jnp.sum(earlier.astype(jnp.int32), axis=1)
    source_pages = jnp.take(prefix_cache_store, send_slot, axis=0)
    page_inner = prefix_cache_store.shape[1:]
    arrived = lax.all_to_all(source_pages, "req", split_axis=0, concat_axis=0, tiled=True)
    chosen = jnp.take(arrived.reshape((req_devices * cap_slots,) + page_inner), flat_pick, axis=0)
    prefix_cols = jax.vmap(window_cols)(chosen, my_fill)
    prefix = jnp.transpose(prefix_cols, (0, 3, 1, 2))
    key_all = jnp.concatenate(
        [key_rows, prefix[:, :, 0].reshape(req_per_dev * WINDOW, head_column_set)], axis=0
    )
    value_all = jnp.concatenate(
        [value_row_block, prefix[:, :, 1].reshape(req_per_dev * WINDOW, head_column_set)], axis=0
    )
    distance = positions[:, None] - positions[None, :]
    local_ok = (request_of[:, None] == request_of[None, :]) & (distance >= 0) & (distance <= WINDOW)
    key_request = jnp.repeat(jnp.arange(req_per_dev, dtype=jnp.int32), WINDOW)
    key_offset = jnp.tile(jnp.arange(WINDOW, dtype=jnp.int32), req_per_dev)
    prefix_ok = (request_of[:, None] == key_request[None, :]) & (
        key_offset[None, :] >= relative[:, None]
    )
    allowed = jnp.concatenate([local_ok, prefix_ok], axis=1)
    query_heads = query_rows.reshape(tok_count, head_local, HEAD_SIZE)
    key_heads = key_all.reshape(-1, head_local, HEAD_SIZE)
    value_heads = value_all.reshape(-1, head_local, HEAD_SIZE)
    scores = jnp.einsum(
        "thd,shd->hts", query_heads, key_heads, preferred_element_type=jnp.float32
    ) * (1.0 / math.sqrt(HEAD_SIZE))
    masked = jnp.where(allowed[None], scores, -1e30)
    row_max = jnp.max(masked, axis=-1, keepdims=True)
    exp_scores = jnp.exp(masked - row_max)
    weights = (exp_scores / jnp.sum(exp_scores, axis=-1, keepdims=True)).astype(jnp.bfloat16)
    mixed = (
        jnp.einsum("hts,shd->thd", weights, value_heads, preferred_element_type=jnp.float32)
        .astype(jnp.bfloat16)
        .reshape(tok_count, head_column_set)
    )
    attn_part = (
        jnp.dot(mixed, head_output_weight, preferred_element_type=jnp.float32)
        .astype(jnp.bfloat16)
        .astype(jnp.float32)
    )
    gain_wide = feedforward_norm_gain.astype(jnp.float32)[None, :]
    attn_full = lax.psum(attn_part.astype(jnp.bfloat16), "mdl").astype(jnp.float32)
    resid_full = (stream.astype(jnp.float32) + attn_full).astype(jnp.bfloat16)
    resid_wide = resid_full.astype(jnp.float32)
    mean_sq = jnp.mean(resid_wide * resid_wide, axis=1, keepdims=True)
    normed = (resid_wide * lax.rsqrt(mean_sq + 1e-06) * gain_wide).astype(jnp.bfloat16)
    resid_mine = lax.dynamic_slice_in_dim(resid_full, mdl_index * row_share, row_share, 0)
    full_mlp = lax.all_gather(feedforward_weight, "req", axis=1, tiled=True)
    gate_part = jnp.dot(normed, full_mlp[0], preferred_element_type=jnp.float32)
    up_part = jnp.dot(normed, full_mlp[1], preferred_element_type=jnp.float32)
    hidden = (jax.nn.silu(gate_part) * up_part).astype(jnp.bfloat16)
    mlp_part = (
        jnp.einsum("tf,df->td", hidden, full_mlp[2], preferred_element_type=jnp.float32)
        .astype(jnp.bfloat16)
        .astype(jnp.float32)
    )
    mlp_mine = lax.psum_scatter(
        mlp_part.astype(jnp.bfloat16), "mdl", scatter_dimension=0, tiled=True
    ).astype(jnp.float32)
    return (resid_mine.astype(jnp.float32) + mlp_mine).astype(jnp.bfloat16)


def solution(mesh):
    return jax.shard_map(
        per_device,
        mesh=mesh,
        in_specs=(
            P("req", None),
            P(None, "mdl", None),
            P("mdl", None),
            P("mdl", None, None),
            P(None, "mdl", None),
            P(),
            P(),
            P(None, "req", "mdl"),
            P("req", None, "mdl", None),
            P("req"),
            P("req", None),
            P("req"),
            P(),
            P(),
            P(),
        ),
        out_specs=P(("req", "mdl"), None),
        check_vma=False,
    )
```

profile of v0, /device:TPU:8, one launch (start us, length us, event | category | flops | bytes accessed | tf_op | source)
XLA Modules:
  0.0 413.7 jit_solution(9208175052067111481)
XLA Ops:
  7.4 0.8 fusion.34
  8.4 0.2 reduce_window_sum.18
  8.6 0.8 mul.153
  9.5 0.1 copy.34
  9.6 0.1 reshape.179
  9.8 0.1 copy.33
  9.9 6.5 %gather_fusion = bf16[64,2,224,128]{3,2,1,0:T(8,128)(2,1)} fusion(bf16[32,2,224,128]{3,2,1,0:T(8,128)(2,1)} %param.23, s32[1024]{0:T(1024)S(1)} %pad_clamp_fusion.1), kind=kCustom, calls=%fused_computation | custom fusion | bytes 14680320 | tf_op jit(solution)/shard_map/jit(_take)/gather | solution.py:101
  16.4 6.9 %broadcast_select_fusion = bf16[32,2,2,224,128]{4,3,2,1,0:T(8,128)(2,1)} fusion(bf16[32,2,2,224,128]{4,3,2,1,0:T(8,128)(2,1)} %bitcast.74, pred[32,2]{1,0:T(8,128)(4,1)S(1)} %copy.33), kind=kLoop, calls=%fused_computation.8 | loop fusion | flops 3670016 | bytes 14680128 | tf_op jit(solution)/shard_map/jit(_take)/select_n | solution.py:101
  23.2 11.9 %all-to-all-start = ((bf16[32,2,2,224,128]{4,3,2,1,0:T(8,128)(2,1)}), bf16[32,2,2,224,128]{4,3,2,1,0:T(8,128)(2,1)}, u32[]{:S(2)}, u32[]{:S(2)}) async-start(bf16[32,2,2,224,128]{4,3,2,1,0:T(8,128)(2,1)} %broadcast_select_fusion), calls=%async_computation | async-start | bytes 14680064 | tf_op jit(solution)/shard_map/all_to_all | solution.py:103
  35.3 0.1 reduce
  35.6 3.9 fusion.17
  39.5 1.3 copy-done.2
  41.0 2.8 fusion.50
  43.8 26.7 %psum.14 = bf16[768,16]{0,1:T(8,128)(2,1)S(1)} all-reduce(bf16[768,16]{0,1:T(8,128)(2,1)S(1)} %multiply_reduce_fusion), channel_id=1, replica_groups=mesh['req'=32,'mdl'=8] {'mdl'}, use_global_device_ids=true, to_apply=%region_4.5 | all-reduce | flops 12288 | bytes 49152 | tf_op jit(solution)/shard_map/psum | solution.py:58
  70.5 0.8 fusion.37
  71.3 0.2 convert_reduce_fusion
  71.5 0.8 and_bitcast_fusion
  72.4 0.1 select_reduce_fusion.2
  72.5 0.1 select_reduce_fusion.1
  72.6 0.1 broadcast_multiply_fusion
  72.7 1.4 fusion.47
  74.1 2.1 fusion.51
  76.2 0.1 fusion.48
  76.3 0.3 fusion.14
  76.6 1.0 add_convert_fusion.3
  77.7 1.2 compare_and_fusion
  79.0 1.4 pad_add_fusion
  80.3 118.6 %all-to-all-done = bf16[32,2,2,224,128]{4,3,2,1,0:T(8,128)(2,1)} async-done(((bf16[32,2,2,224,128]{4,3,2,1,0:T(8,128)(2,1)}), bf16[32,2,2,224,128]{4,3,2,1,0:T(8,128)(2,1)}, u32[]{:S(2)}, u32[]{:S(2)}) %all-to-all-start) | async-done | bytes 7340064 | tf_op jit(solution)/shard_map/all_to_all | solution.py:103
  198.9 5.7 %gather_fusion.1 = bf16[24,2,224,128]{3,2,1,0:T(8,128)(2,1)} fusion(bf16[64,2,224,128]{3,2,1,0:T(8,128)(2,1)} %bitcast.16, s32[1024]{0:T(1024)S(1)} %pad_clamp_fusion), kind=kCustom, calls=%fused_computation.1 | custom fusion | bytes 5505120 | tf_op jit(solution)/shard_map/jit(_take)/gather | solution.py:104
  204.6 3.7 broadcast_select_fusion.1
  208.3 8.8 %copy.35 = bf16[24,2,224,128]{2,1,0,3:T(2,128)(2,1)} copy(bf16[24,2,224,128]{3,2,1,0:T(8,128)(2,1)} %broadcast_select_fusion.1) | data formatting | bytes 5505024 | tf_op jit(solution)/shard_map/jit(_take)/select_n | solution.py:104
  217.1 8.9 %gather_fusion.2 = bf16[24,2,224,64]{2,1,3,0:T(2,128)(2,1)S(1)} fusion(bf16[24,2,224,128]{2,1,0,3:T(2,128)(2,1)} %copy.35, s32[24]{0:T(128)S(1)} %get-tuple-element.21), kind=kCustom, calls=%fused_computation.2 | custom fusion | bytes 2752896 | tf_op jit(solution)/shard_map/vmap()/gather | solution.py:12
  226.0 6.5 %slice_reduce_fusion.1 = (bf16[24,64,224]{2,1,0:T(8,128)(2,1)S(1)}, bf16[24,64,224]{2,1,0:T(8,128)(2,1)S(1)}) fusion(bf16[24,64,2,224]{3,2,1,0:T(2,128)(2,1)S(1)} %bitcast.75), kind=kLoop, calls=%fused_computation.40 | loop fusion | bytes 2752512 | tf_op jit(solution)/shard_map/slice | solution.py:111
  232.5 0.4 concatenate.23
  232.9 0.6 copy.37
  233.5 0.4 concatenate.20
  233.9 0.6 copy.36
  234.5 9.7 %fusion.49 = (f32[2,768]{1,0:T(2,128)S(1)}, f32[2,768,2304]{2,1,0:T(8,128)}) fusion(pred[768,2304]{1,0:T(8,128)(4,1)} %pad_add_fusion, bf16[768,2,112]{0,2,1:T(8,128)(2,1)S(1)} %copy-done.6, bf16[1536,2,112]{0,2,1:T(8,128)(2,1)S(1)} %copy.37, bf16[768,2,112]{0,2,1:T(8,128)(2,1)S(1)} %bitcast.83), kind=kOutput, calls=%fused_computation.100 | convolution fusion | flops 808945920 | bytes 17307648 | tf_op jit(solution)/shard_map/sub | solution.py:129
  244.2 7.6 %fusion.22 = bf16[2,112,768]{2,1,0:T(8,128)(2,1)S(1)} fusion(f32[2,768,2304]{2,1,0:T(8,128)} %get-tuple-element.20, f32[2,768]{1,0:T(2,128)S(1)} %get-tuple-element.19, bf16[1536,2,112]{0,2,1:T(8,128)(2,1)S(1)} %copy.36, bf16[768,2,112]{0,2,1:T(8,128)(2,1)S(1)} %copy-done.5), kind=kOutput, calls=%fused_computation.41 | convolution fusion | flops 802037760 | bytes 15538176 | tf_op jit(solution)/shard_map/hts,shd->thd/dot_general | solution.py:132
  251.8 2.5 convolution_convert_fusion
  254.4 0.5 all-gather.2.cloned.1.call-update
  255.0 77.6 %all-reduce.3.cloned.1.call-done = bf16[768,1792]{1,0:T(8,128)(2,1)} async-done(((bf16[768,1792]{1,0:T(8,128)(2,1)}), bf16[768,1792]{1,0:T(8,128)(2,1)}) %all-reduce.3.cloned.1.call-update) | async-done | bytes 2752528 | tf_op jit(solution)/shard_map/psum | solution.py:142
  332.6 5.3 %fusion.6 = (f32[768]{0:T(1024)S(1)}, bf16[768,1792]{1,0:T(8,128)(2,1)}) fusion(bf16[768,1792]{1,0:T(8,128)(2,1)} %all-reduce.3.cloned.1.call-done, bf16[768,1792]{1,0:T(8,128)(2,1)} %param.15), kind=kLoop, calls=%fused_computation.16 | loop fusion | flops 9633024 | bytes 8260608 | tf_op jit(solution)/shard_map/reduce_sum | solution.py:145
  338.0 14.1 %all-gather.2.cloned.1.call-done = bf16[3,1792,608]{2,1,0:T(8,128)(2,1)} async-done(((bf16[3,56,608]{2,1,0:T(8,128)(2,1)}), bf16[3,1792,608]{2,1,0:T(8,128)(2,1)}) %all-gather.2.cloned.1.call-update) | async-done | bytes 6537232 | tf_op jit(solution)/shard_map/all_gather | solution.py:148
  352.0 5.8 %fusion.16 = f32[768,608]{0,1:T(8,128)} fusion(bf16[3,1792,608]{2,1,0:T(8,128)(2,1)} %all-gather.2.cloned.1.call-done, bf16[768,1792]{1,0:T(8,128)(2,1)} %get-tuple-element.10, f32[1792]{0:T(1024)S(1)} %convert_element_type.118, f32[768]{0:T(1024)S(1)} %add_rsqrt_fusion), kind=kOutput, calls=%fused_computation.35 | convolution fusion | flops 1679032320 | bytes 6924288 | tf_op jit(solution)/shard_map/dot_general | solution.py:149
  357.9 10.5 %convolution_convert_fusion.1 = bf16[768,1792]{1,0:T(8,128)(2,1)} fusion(bf16[3,1792,608]{2,1,0:T(8,128)(2,1)} %all-gather.2.cloned.1.call-done, f32[768,608]{0,1:T(8,128)} %fusion.16, bf16[768,1792]{1,0:T(8,128)(2,1)} %get-tuple-element.10, f32[1792]{0:T(1024)S(1)} %convert_element_type.118, f32[768]{0:T(1024)S(1)} %add_rsqrt_fusion), kind=kOutput, calls=%fused_computation.22 | convolution fusion | flops 3356737536 | bytes 11970560 | tf_op jit(solution)/shard_map/tf,df->td/dot_general | solution.py:153
  368.5 36.0 %reduce-scatter.2.cloned.1.call-done = bf16[96,1792]{1,0:T(8,128)(2,1)} async-done(((bf16[768,1792]{1,0:T(8,128)(2,1)}), bf16[96,1792]{1,0:T(8,128)(2,1)}) %reduce-scatter.2.cloned.1.call-update) | async-done | bytes 344080 | tf_op jit(solution)/shard_map/reduce_scatter | solution.py:157
  404.4 1.9 add_convert_fusion.1
  (54 shorter events, 1.1 us)
Async XLA Ops:
  7.4 28.2 %copy-start = (bf16[3,224,1792]{2,1,0:T(8,128)(2,1)S(1)}, bf16[3,224,1792]{2,1,0:T(8,128)(2,1)}, u32[]{:S(2)}) copy-start(bf16[3,224,1792]{2,1,0:T(8,128)(2,1)} %param.16) | copy-start | bytes 7225348
  23.2 11.9 %copy-start.9 = (s32[1,24]{1,0:T(1,128)S(1)}, s32[1,24]{1,0:T(1,128)}, u32[]{:S(2)}) copy-start(s32[1,24]{1,0:T(1,128)} %param.25) | copy-start | bytes 292
  23.2 175.7 %all-to-all-start = ((bf16[32,2,2,224,128]{4,3,2,1,0:T(8,128)(2,1)}), bf16[32,2,2,224,128]{4,3,2,1,0:T(8,128)(2,1)}, u32[]{:S(2)}, u32[]{:S(2)}) async-start(bf16[32,2,2,224,128]{4,3,2,1,0:T(8,128)(2,1)} %broadcast_select_fusion), calls=%async_computation | async-start | bytes 14680064 | tf_op jit(solution)/shard_map/all_to_all | solution.py:103
  35.1 297.5 %all-reduce.3.cloned.1.call-start = ((), (), s32[]{:S(2)}) async-start(), calls=%async_computation.2 | async-start | bytes 5505024 | tf_op jit(solution)/shard_map/psum | solution.py:142
  35.6 5.3 %copy-start.7 = (s32[768]{0:T(1024)S(1)}, s32[768]{0:T(1024)}, u32[]{:S(2)}) copy-start(s32[768]{0:T(1024)} %param.24) | copy-start | bytes 9220
  35.6 5.4 %copy-start.4 = (bf16[8,1792,16]{1,2,0:T(8,128)(2,1)S(1)}, bf16[8,1792,16]{1,2,0:T(8,128)(2,1)}, u32[]{:S(2)}) copy-start(bf16[8,1792,16]{1,2,0:T(8,128)(2,1)} %param.18) | copy-start | bytes 1376260
  39.5 1.3 copy-start.2
  40.9 31.4 %copy-start.10 = (f32[4]{0:T(128)S(1)}, f32[4]{0:T(128)}, u32[]{:S(2)}) copy-start(f32[4]{0:T(128)} %param.20) | copy-start | bytes 52
  40.9 31.4 %copy-start.11 = (s32[24]{0:T(128)S(1)}, s32[24]{0:T(128)}, u32[]{:S(2)}) copy-start(s32[24]{0:T(128)} %param.26) | copy-start | bytes 292
  232.9 1.6 copy-start.6
  234.5 9.8 %copy-start.5 = (bf16[768,2,112]{0,2,1:T(8,128)(2,1)S(1)}, bf16[768,2,112]{0,2,1:T(8,128)(2,1)}, u32[]{:S(2)}) copy-start(bf16[768,2,112]{0,2,1:T(8,128)(2,1)} %get-tuple-element.17) | copy-start | bytes 1032196
  244.2 7.6 %copy-start.3 = (bf16[224,1792]{1,0:T(8,128)(2,1)S(1)}, bf16[224,1792]{1,0:T(8,128)(2,1)}, u32[]{:S(2)}) copy-start(bf16[224,1792]{1,0:T(8,128)(2,1)} %param.17) | copy-start | bytes 2408452
  251.8 3.2 copy-start.8
  254.4 97.6 %all-gather.2.cloned.1.call-start = ((), (), s32[]{:S(2)}) async-start(), calls=%async_computation.3 | async-start | bytes 7096320 | tf_op jit(solution)/shard_map/all_gather | solution.py:148
  255.0 149.4 %reduce-scatter.2.cloned.1.call-start = ((), (), s32[]{:S(2)}) async-start(), calls=%async_computation.4 | async-start | bytes 3096576 | tf_op jit(solution)/shard_map/reduce_scatter | solution.py:157
  357.9 48.4 %copy-start.1 = (bf16[3,224,1792]{2,1,0:T(8,128)(2,1)S(1)}, bf16[3,224,1792]{2,1,0:T(8,128)(2,1)}, u32[]{:S(2)}) copy-start(bf16[3,224,1792]{2,1,0:T(8,128)(2,1)} %param.16) | copy-start | bytes 7225348
Sparse Core Ops, SparseCore 0:
  254.5 78.0 all-reduce.2
  368.6 35.7 reduce-scatter.1
Sparse Core Ops, SparseCore 1:
  257.9 94.1 all-gather.1
where the time goes:
time: 415 us; the launch traced here: 414 us
  waiting for transfers between devices  247 us (60%)
  matrix products  45 us (11%)
  local copies, waits for them, and re-layouts  42.8 us (10%)
  blocking collectives  26.7 us (6%)
  other arithmetic  25.3 us (6%)
  between operations  15.2 us (4%)
  starting transfers between devices  12 us (3%)
    all_to_all x1, waiting for transfers between devices, per_device(): lax.all_to_all(source_pages, 'req', split_axis=0, concat_axis=0, tiled=True)  119 us
    psum x1, waiting for transfers between devices, per_device(): lax.psum(attn_part.astype(jnp.bfloat16), 'mdl').astype(jnp.float32)  77.6 us
    reduce_scatter x1, waiting for transfers between devices, per_device(): lax.psum_scatter(mlp_part.astype(jnp.bfloat16), 'mdl', scatter_dimension=...  36 us
    psum x1, blocking collectives, per_device(): rank_feat = lax.psum(rank_part.astype(jnp.bfloat16), 'mdl')  26.7 us
    all_gather x1, waiting for transfers between devices, per_device(): full_mlp = lax.all_gather(feedforward_weight, 'req', axis=1, tiled=True)  14.1 us
    all_to_all x1, starting transfers between devices, per_device(): lax.all_to_all(source_pages, 'req', split_axis=0, concat_axis=0, tiled=True)  11.9 us
    dot_general x1, matrix products, per_device(): jnp.einsum('tf,df->td', hidden, full_mlp[2], preferred_element_type=jnp.f...  10.5 us
    sub x1, matrix products, per_device(): exp_scores = jnp.exp(masked - row_max)  9.74 us
  transfers between devices with their start and end apart: 4, of which 4 were waited for; matrix products, arithmetic and copies ran while one was open for 5% of the time, Pallas kernels for 0%

commit v1 on v0

--- a/solution.py
+++ b/solution.py
@@ -139,7 +139,11 @@
         .astype(jnp.float32)
     )
     gain_wide = feedforward_norm_gain.astype(jnp.float32)[None, :]
-    attn_full = lax.psum(attn_part.astype(jnp.bfloat16), "mdl").astype(jnp.float32)
+
+    def build_cycles(s0, dev_axis):
+        return jax.lax.all_gather(s0, dev_axis).sum(axis=0)
+
+    attn_full = build_cycles(attn_part.astype(jnp.bfloat16), "mdl").astype(jnp.float32)
     resid_full = (stream.astype(jnp.float32) + attn_full).astype(jnp.bfloat16)
     resid_wide = resid_full.astype(jnp.float32)
     mean_sq = jnp.mean(resid_wide * resid_wide, axis=1, keepdims=True)

time: 415 us -> 523 us (1.26)
  waiting for transfers between devices: 247 us -> 343 us
  other arithmetic: 25.3 us -> 39.2 us
    all_gather x0 -> x1, waiting for transfers between devices: none -> 113 us  [build_cycles(): return jax.lax.all_gather(s0, dev_axis).sum(axis=0)]
    psum x1 -> x0, waiting for transfers between devices: 77.6 us -> none  [per_device(): lax.psum(attn_part.astype(jnp.bfloat16), 'mdl').astype(jnp.float32)]
    all_gather x1, waiting for transfers between devices: 14.1 us -> 74.3 us  [per_device(): full_mlp = lax.all_gather(feedforward_weight, 'req', axis=1, tiled=True)]
    reduce_sum x0 -> x1, other arithmetic: none -> 14 us  [build_cycles(): return jax.lax.all_gather(s0, dev_axis).sum(axis=0)]
  transfers between devices with their start and end apart: 4 -> 4, of which waited for: 4 -> 4; matrix products, arithmetic and copies ran while one was open for 5% -> 7% of each run, Pallas kernels for 0% -> 0%
where the time goes in v1:
time: 523 us; the launch traced here: 522 us
  waiting for transfers between devices  343 us (66%)
  matrix products  44.9 us (9%)
  local copies, waits for them, and re-layouts  42.8 us (8%)
  other arithmetic  39.2 us (7%)
  blocking collectives  26.7 us (5%)
  between operations  13.5 us (3%)
  starting transfers between devices  12 us (2%)
    all_to_all x1, waiting for transfers between devices, per_device(): lax.all_to_all(source_pages, 'req', split_axis=0, concat_axis=0, tiled=True)  119 us
    all_gather x1, waiting for transfers between devices, build_cycles(): return jax.lax.all_gather(s0, dev_axis).sum(axis=0)  113 us
    all_gather x1, waiting for transfers between devices, per_device(): full_mlp = lax.all_gather(feedforward_weight, 'req', axis=1, tiled=True)  74.3 us
    reduce_scatter x1, waiting for transfers between devices, per_device(): lax.psum_scatter(mlp_part.astype(jnp.bfloat16), 'mdl', scatter_dimension=...  36.2 us
    psum x1, blocking collectives, per_device(): rank_feat = lax.psum(rank_part.astype(jnp.bfloat16), 'mdl')  26.7 us
    reduce_sum x1, other arithmetic, build_cycles(): return jax.lax.all_gather(s0, dev_axis).sum(axis=0)  14 us
    all_to_all x1, starting transfers between devices, per_device(): lax.all_to_all(source_pages, 'req', split_axis=0, concat_axis=0, tiled=True)  11.9 us
    dot_general x1, matrix products, per_device(): jnp.einsum('tf,df->td', hidden, full_mlp[2], preferred_element_type=jnp.f...  10.6 us
  transfers between devices with their start and end apart: 4, of which 4 were waited for; matrix products, arithmetic and copies ran while one was open for 7% of the time, Pallas kernels for 0%

profile of v1, /device:TPU:8, one launch (start us, length us, event | category | flops | bytes accessed | tf_op | source)
XLA Modules:
  0.0 521.9 jit_solution(5590706551452549553)
XLA Ops:
  6.5 0.8 fusion.34
  7.5 0.2 reduce_window_sum.18
  7.8 0.8 mul.153
  8.8 0.1 reshape.179
  8.9 0.1 copy.33
  9.0 6.5 %gather_fusion = bf16[64,2,224,128]{3,2,1,0:T(8,128)(2,1)} fusion(bf16[32,2,224,128]{3,2,1,0:T(8,128)(2,1)} %param.23, s32[1024]{0:T(1024)S(1)} %pad_clamp_fusion.1), kind=kCustom, calls=%fused_computation | custom fusion | bytes 14680320 | tf_op jit(solution)/shard_map/jit(_take)/gather | solution.py:101
  15.5 6.9 %broadcast_select_fusion = bf16[32,2,2,224,128]{4,3,2,1,0:T(8,128)(2,1)} fusion(bf16[32,2,2,224,128]{4,3,2,1,0:T(8,128)(2,1)} %bitcast.75, pred[32,2]{1,0:T(8,128)(4,1)S(1)} %copy.33), kind=kLoop, calls=%fused_computation.8 | loop fusion | flops 3670016 | bytes 14680128 | tf_op jit(solution)/shard_map/jit(_take)/select_n | solution.py:101
  22.4 11.9 %all-to-all-start = ((bf16[32,2,2,224,128]{4,3,2,1,0:T(8,128)(2,1)}), bf16[32,2,2,224,128]{4,3,2,1,0:T(8,128)(2,1)}, u32[]{:S(2)}, u32[]{:S(2)}) async-start(bf16[32,2,2,224,128]{4,3,2,1,0:T(8,128)(2,1)} %broadcast_select_fusion), calls=%async_computation | async-start | bytes 14680064 | tf_op jit(solution)/shard_map/all_to_all | solution.py:103
  34.5 0.1 reduce.1
  34.8 3.9 fusion.17
  38.7 1.3 copy-done.2
  40.2 2.8 fusion.50
  43.0 26.7 %psum.7 = bf16[768,16]{0,1:T(8,128)(2,1)S(1)} all-reduce(bf16[768,16]{0,1:T(8,128)(2,1)S(1)} %multiply_reduce_fusion), channel_id=1, replica_groups=mesh['req'=32,'mdl'=8] {'mdl'}, use_global_device_ids=true, to_apply=%region_4.5 | all-reduce | flops 12288 | bytes 49152 | tf_op jit(solution)/shard_map/psum | solution.py:58
  69.7 0.8 fusion.37
  70.5 0.2 convert_reduce_fusion
  70.6 0.8 and_bitcast_fusion
  71.5 0.1 select_reduce_fusion.2
  71.6 0.1 select_reduce_fusion.1
  71.8 0.1 broadcast_multiply_fusion
  71.9 1.4 fusion.47
  73.3 2.1 fusion.51
  75.4 0.1 fusion.48
  75.5 0.3 fusion.14
  75.8 1.0 add_convert_fusion.3
  76.8 1.2 compare_and_fusion
  78.1 1.4 pad_add_fusion
  79.5 118.6 %all-to-all-done = bf16[32,2,2,224,128]{4,3,2,1,0:T(8,128)(2,1)} async-done(((bf16[32,2,2,224,128]{4,3,2,1,0:T(8,128)(2,1)}), bf16[32,2,2,224,128]{4,3,2,1,0:T(8,128)(2,1)}, u32[]{:S(2)}, u32[]{:S(2)}) %all-to-all-start) | async-done | bytes 7340064 | tf_op jit(solution)/shard_map/all_to_all | solution.py:103
  198.1 5.7 %gather_fusion.1 = bf16[24,2,224,128]{3,2,1,0:T(8,128)(2,1)} fusion(bf16[64,2,224,128]{3,2,1,0:T(8,128)(2,1)} %bitcast.16, s32[1024]{0:T(1024)S(1)} %pad_clamp_fusion), kind=kCustom, calls=%fused_computation.1 | custom fusion | bytes 5505120 | tf_op jit(solution)/shard_map/jit(_take)/gather | solution.py:104
  203.8 3.7 broadcast_select_fusion.1
  207.5 8.8 %copy.35 = bf16[24,2,224,128]{2,1,0,3:T(2,128)(2,1)} copy(bf16[24,2,224,128]{3,2,1,0:T(8,128)(2,1)} %broadcast_select_fusion.1) | data formatting | bytes 5505024 | tf_op jit(solution)/shard_map/jit(_take)/select_n | solution.py:104
  216.2 8.9 %gather_fusion.2 = bf16[24,2,224,64]{2,1,3,0:T(2,128)(2,1)S(1)} fusion(bf16[24,2,224,128]{2,1,0,3:T(2,128)(2,1)} %copy.35, s32[24]{0:T(128)S(1)} %get-tuple-element.21), kind=kCustom, calls=%fused_computation.2 | custom fusion | bytes 2752896 | tf_op jit(solution)/shard_map/vmap()/gather | solution.py:12
  225.1 6.5 %slice_reduce_fusion.1 = (bf16[24,64,224]{2,1,0:T(8,128)(2,1)S(1)}, bf16[24,64,224]{2,1,0:T(8,128)(2,1)S(1)}) fusion(bf16[24,64,2,224]{3,2,1,0:T(2,128)(2,1)S(1)} %bitcast.76), kind=kLoop, calls=%fused_computation.40 | loop fusion | bytes 2752512 | tf_op jit(solution)/shard_map/slice | solution.py:111
  231.6 0.4 concatenate.23
  232.0 0.6 copy.37
  232.6 0.4 concatenate.20
  233.0 0.6 copy.36
  233.7 9.7 %fusion.49 = (f32[2,768]{1,0:T(2,128)S(1)}, f32[2,768,2304]{2,1,0:T(8,128)}) fusion(pred[768,2304]{1,0:T(8,128)(4,1)} %pad_add_fusion, bf16[768,2,112]{0,2,1:T(8,128)(2,1)S(1)} %copy-done.6, bf16[1536,2,112]{0,2,1:T(8,128)(2,1)S(1)} %copy.37, bf16[768,2,112]{0,2,1:T(8,128)(2,1)S(1)} %bitcast.85), kind=kOutput, calls=%fused_computation.100 | convolution fusion | flops 808945920 | bytes 17307648 | tf_op jit(solution)/shard_map/sub | solution.py:129
  243.4 7.6 %fusion.22 = bf16[2,112,768]{2,1,0:T(8,128)(2,1)S(1)} fusion(f32[2,768,2304]{2,1,0:T(8,128)} %get-tuple-element.20, f32[2,768]{1,0:T(2,128)S(1)} %get-tuple-element.19, bf16[1536,2,112]{0,2,1:T(8,128)(2,1)S(1)} %copy.36, bf16[768,2,112]{0,2,1:T(8,128)(2,1)S(1)} %copy-done.5), kind=kOutput, calls=%fused_computation.41 | convolution fusion | flops 802037760 | bytes 15538176 | tf_op jit(solution)/shard_map/hts,shd->thd/dot_general | solution.py:132
  251.0 2.5 convolution_convert_fusion
  253.6 0.7 all-gather.4.cloned.1.call-update
  254.3 113.1 %all-gather.6.cloned.1.call-done = bf16[6144,1792]{1,0:T(8,128)(2,1)} async-done(((bf16[768,1792]{1,0:T(8,128)(2,1)}), bf16[6144,1792]{1,0:T(8,128)(2,1)}) %all-gather.6.cloned.1.call-update) | async-done | bytes 22020112 | tf_op jit(solution)/shard_map/all_gather | solution.py:144
  367.4 14.0 %reduce_sum.107 = bf16[768,1792]{1,0:T(8,128)(2,1)} reduce(bf16[8,768,1792]{2,1,0:T(8,128)(2,1)} %bitcast.77, bf16[]{:T(256)} %constant.87.clone.1), dimensions={0}, to_apply=%region_12.13 | reduce | flops 9633792 | bytes 24772610 | tf_op jit(solution)/shard_map/reduce_sum | solution.py:144
  381.4 5.3 %fusion.6 = (f32[768]{0:T(1024)S(1)}, bf16[768,1792]{1,0:T(8,128)(2,1)}) fusion(bf16[768,1792]{1,0:T(8,128)(2,1)} %reduce_sum.107, bf16[768,1792]{1,0:T(8,128)(2,1)} %param.15), kind=kLoop, calls=%fused_computation.16 | loop fusion | flops 9633024 | bytes 8260608 | tf_op jit(solution)/shard_map/reduce_sum | solution.py:149
  386.6 74.3 %all-gather.4.cloned.1.call-done = bf16[3,1792,608]{2,1,0:T(8,128)(2,1)} async-done(((bf16[3,56,608]{2,1,0:T(8,128)(2,1)}), bf16[3,1792,608]{2,1,0:T(8,128)(2,1)}) %all-gather.4.cloned.1.call-update) | async-done | bytes 6537232 | tf_op jit(solution)/shard_map/all_gather | solution.py:152
  460.9 5.8 %fusion.16 = f32[768,608]{0,1:T(8,128)} fusion(bf16[3,1792,608]{2,1,0:T(8,128)(2,1)} %all-gather.4.cloned.1.call-done, bf16[768,1792]{1,0:T(8,128)(2,1)} %get-tuple-element.10, f32[1792]{0:T(1024)S(1)} %convert_element_type.120, f32[768]{0:T(1024)S(1)} %add_rsqrt_fusion), kind=kOutput, calls=%fused_computation.35 | convolution fusion | flops 1679032320 | bytes 6924288 | tf_op jit(solution)/shard_map/dot_general | solution.py:153
  466.7 10.6 %convolution_convert_fusion.1 = bf16[768,1792]{1,0:T(8,128)(2,1)} fusion(bf16[3,1792,608]{2,1,0:T(8,128)(2,1)} %all-gather.4.cloned.1.call-done, f32[768,608]{0,1:T(8,128)} %fusion.16, bf16[768,1792]{1,0:T(8,128)(2,1)} %get-tuple-element.10, f32[1792]{0:T(1024)S(1)} %convert_element_type.120, f32[768]{0:T(1024)S(1)} %add_rsqrt_fusion), kind=kOutput, calls=%fused_computation.22 | convolution fusion | flops 3356737536 | bytes 11970560 | tf_op jit(solution)/shard_map/tf,df->td/dot_general | solution.py:157
  477.3 36.2 %reduce-scatter.2.cloned.1.call-done = bf16[96,1792]{1,0:T(8,128)(2,1)} async-done(((bf16[768,1792]{1,0:T(8,128)(2,1)}), bf16[96,1792]{1,0:T(8,128)(2,1)}) %reduce-scatter.2.cloned.1.call-update) | async-done | bytes 344080 | tf_op jit(solution)/shard_map/reduce_scatter | solution.py:161
  513.5 1.9 add_convert_fusion.1
  (55 shorter events, 1.2 us)
Async XLA Ops:
  6.5 28.2 %copy-start = (bf16[3,224,1792]{2,1,0:T(8,128)(2,1)S(1)}, bf16[3,224,1792]{2,1,0:T(8,128)(2,1)}, u32[]{:S(2)}) copy-start(bf16[3,224,1792]{2,1,0:T(8,128)(2,1)} %param.16) | copy-start | bytes 7225348
  22.4 11.9 %copy-start.9 = (s32[1,24]{1,0:T(1,128)S(1)}, s32[1,24]{1,0:T(1,128)}, u32[]{:S(2)}) copy-start(s32[1,24]{1,0:T(1,128)} %param.25) | copy-start | bytes 292
  22.4 175.7 %all-to-all-start = ((bf16[32,2,2,224,128]{4,3,2,1,0:T(8,128)(2,1)}), bf16[32,2,2,224,128]{4,3,2,1,0:T(8,128)(2,1)}, u32[]{:S(2)}, u32[]{:S(2)}) async-start(bf16[32,2,2,224,128]{4,3,2,1,0:T(8,128)(2,1)} %broadcast_select_fusion), calls=%async_computation | async-start | bytes 14680064 | tf_op jit(solution)/shard_map/all_to_all | solution.py:103
  34.3 333.1 %all-gather.6.cloned.1.call-start = ((), (), s32[]{:S(2)}) async-start(), calls=%async_computation.4 | async-start | bytes 24772608 | tf_op jit(solution)/shard_map/all_gather | solution.py:144
  34.8 5.3 %copy-start.7 = (s32[768]{0:T(1024)S(1)}, s32[768]{0:T(1024)}, u32[]{:S(2)}) copy-start(s32[768]{0:T(1024)} %param.24) | copy-start | bytes 9220
  34.8 5.4 %copy-start.4 = (bf16[8,1792,16]{1,2,0:T(8,128)(2,1)S(1)}, bf16[8,1792,16]{1,2,0:T(8,128)(2,1)}, u32[]{:S(2)}) copy-start(bf16[8,1792,16]{1,2,0:T(8,128)(2,1)} %param.18) | copy-start | bytes 1376260
  38.7 1.3 copy-start.2
  40.0 31.4 %copy-start.10 = (f32[4]{0:T(128)S(1)}, f32[4]{0:T(128)}, u32[]{:S(2)}) copy-start(f32[4]{0:T(128)} %param.20) | copy-start | bytes 52
  40.0 31.4 %copy-start.11 = (s32[24]{0:T(128)S(1)}, s32[24]{0:T(128)}, u32[]{:S(2)}) copy-start(s32[24]{0:T(128)} %param.26) | copy-start | bytes 292
  232.0 1.6 copy-start.6
  233.7 9.7 %copy-start.5 = (bf16[768,2,112]{0,2,1:T(8,128)(2,1)S(1)}, bf16[768,2,112]{0,2,1:T(8,128)(2,1)}, u32[]{:S(2)}) copy-start(bf16[768,2,112]{0,2,1:T(8,128)(2,1)} %get-tuple-element.17) | copy-start | bytes 1032196
  243.4 7.6 %copy-start.3 = (bf16[224,1792]{1,0:T(8,128)(2,1)S(1)}, bf16[224,1792]{1,0:T(8,128)(2,1)}, u32[]{:S(2)}) copy-start(bf16[224,1792]{1,0:T(8,128)(2,1)} %param.17) | copy-start | bytes 2408452
  251.0 3.3 copy-start.8
  253.5 207.4 %all-gather.4.cloned.1.call-start = ((), (), s32[]{:S(2)}) async-start(), calls=%async_computation.2 | async-start | bytes 7096320 | tf_op jit(solution)/shard_map/all_gather | solution.py:152
  254.3 259.2 %reduce-scatter.2.cloned.1.call-start = ((), (), s32[]{:S(2)}) async-start(), calls=%async_computation.3 | async-start | bytes 3096576 | tf_op jit(solution)/shard_map/reduce_scatter | solution.py:161
  466.7 48.7 %copy-start.1 = (bf16[3,224,1792]{2,1,0:T(8,128)(2,1)S(1)}, bf16[3,224,1792]{2,1,0:T(8,128)(2,1)}, u32[]{:S(2)}) copy-start(bf16[3,224,1792]{2,1,0:T(8,128)(2,1)} %param.16) | copy-start | bytes 7225348
Sparse Core Ops, SparseCore 0:
  253.6 113.7 all-gather.5
  370.1 90.8 all-gather.3
  477.4 36.0 reduce-scatter.1
